TPU v7x, 32 devices: a whole 2x2x4 slice. The times are simulated.
32 devices in a mesh: rows: 8 (over z, y), cols: 4 (over x, core).
Axes of the slice: x: 2, y: 2, z: 4, core: 2. Of those that a mesh axis runs over, the one named last changes fastest.
Arguments:
- sketch: float32 [32768, 256], P(('rows', 'cols'))
- tiles: bfloat16 [1280, 512, 512], P(('rows', 'cols')), may hold values from -48 to 48
- tile_user: int32 [1280], P(('rows', 'cols')), may hold values from 0 to 7
- tile_item: int32 [1280], P(('rows', 'cols')), may hold values from 0 to 7
- tile_count: int32 [32], P(('rows', 'cols')), may hold values from 5 to 40, as said below
- item_owner: int32 [4, 8], P('cols'), may hold values from 0 to 7, each once within a row
Outputs:
- projected: float32 [8, 4, 256, 512], P('rows', 'cols')
Inputs may be any that keep to these rules, and one draw needn't show every extreme that they name: `tile_count`: live slots of a device are its first slots; some device has all 40 live in every draw.
All inputs are finite; a program needn't handle non-finite values.
Results may differ from a plain program's by a relative error of at most 0.0029.
Values may be sent and summed in bfloat16 or wider, within the bound.
No kernel may reach another device: no remote copies, remote signals or barrier semaphores. Data moves between devices by JAX's collectives and lax.ppermute only.
A program may use at most 192 MiB of HBM per device.

v0:
```python
import jax
import jax.numpy as jnp
from jax import lax
from jax.sharding import PartitionSpec as P


def accumulate(totals, tile_set, users, items, owner, slab, stop, first_row):
    tile_size = tile_set.shape[1]
    row_count = totals.shape[0]

    def step(index, partial_sums):
        target = owner[items[index]] - first_row
        inside = jnp.logical_and(target >= 0, target < row_count)

        def add_tile(sums):
            basis_rows = lax.dynamic_slice_in_dim(slab, users[index] * tile_size, tile_size, 0)
            partial_value = lax.dot_general(
                basis_rows,
                tile_set[index],
                (((0,), (0,)), ((), ())),
                preferred_element_type=jnp.float32,
            )
            place = jnp.clip(target, 0, row_count - 1)
            current = lax.dynamic_index_in_dim(sums, place, 0, keepdims=False)
            return lax.dynamic_update_index_in_dim(sums, current + partial_value, place, 0)

        return lax.cond(inside, add_tile, lambda sums: sums, partial_sums)

    return lax.fori_loop(0, stop, step, totals)


def body(sketch, tiles, tile_user, tile_item, tile_count, item_owner):
    gram = lax.dot_general(
        sketch,
        sketch,
        (((0,), (0,)), ((), ())),
        precision=lax.Precision.HIGHEST,
        preferred_element_type=jnp.float32,
    )
    total = lax.psum(gram, ("rows", "cols"))
    lower_factor = jnp.linalg.cholesky(total)
    basis_full = lax.linalg.triangular_solve(
        lower_factor, sketch, left_side=False, lower=True, transpose_a=True
    )
    basis = basis_full.astype(jnp.bfloat16)
    slab = lax.all_gather(basis, "cols", axis=0, tiled=True)
    owner = item_owner[0]
    live_count = tile_count[0]
    width = sketch.shape[1]
    tile_size = tiles.shape[2]
    totals = jnp.zeros((owner.shape[0], width, tile_size), jnp.float32)
    totals = accumulate(totals, tiles, tile_user, tile_item, owner, slab, live_count, 0)
    owned = lax.psum_scatter(totals, "rows", scatter_dimension=0, tiled=True)
    return owned[:, None]


def solution(mesh):
    placed = (
        P(("rows", "cols"), None),
        P(("rows", "cols"), None, None),
        P(("rows", "cols")),
        P(("rows", "cols")),
        P(("rows", "cols")),
        P("cols", None),
    )
    return jax.shard_map(
        body, mesh=mesh, in_specs=placed, out_specs=P("rows", "cols", None, None), check_vma=False
    )
```

profile of v0, /device:TPU:0, one launch (start us, length us, event | category | flops | bytes accessed | tf_op | source)
XLA Modules:
  0.0 737.1 jit_solution(1801150780538099880)
XLA Ops:
  6.5 4.1 fusion.14
  10.8 129.7 %all-reduce.3.cloned.1.call-done = f32[256,256]{0,1:T(8,128)} async-done(((f32[256,256]{0,1:T(8,128)}), f32[256,256]{0,1:T(8,128)}) %all-reduce.3.cloned.1.call-update) | async-done | bytes 262160 | tf_op jit(solution)/shard_map/psum | solution.py:40
  140.5 1.1 copy.8
  141.6 1.0 fusion.8
  142.6 11.7 %cholesky.50 = f32[128,128]{1,0:T(8,128)S(1)} custom-call(f32[128,128]{1,0:T(8,128)S(1)} %cholesky.118), custom_call_target="Cholesky" | custom-call | tf_op jit(solution)/shard_map/jit(cholesky)/cholesky | solution.py:41
  154.3 9.8 %custom-call.14 = f32[1,128,128]{1,2,0:T(8,128)S(1)} custom-call(f32[1,128,128]{2,1,0:T(8,128)S(1)} %get-tuple-element.116), custom_call_target="InvertDiagBlocksLowerTriangular" | custom-call | tf_op jit(solution)/shard_map/jit(cholesky)/cholesky | solution.py:41
  164.7 11.7 %cholesky.105 = f32[128,128]{1,0:T(8,128)S(1)} custom-call(f32[128,128]{1,0:T(8,128)S(1)} %convolution_subtract_fusion.1), custom_call_target="Cholesky" | custom-call | tf_op jit(solution)/shard_map/jit(cholesky)/cholesky | solution.py:41
  178.4 4.1 while.15
  179.2 1.4 bitcast_dynamic-update-slice_fusion.2
  181.1 1.4 bitcast_dynamic-update-slice_fusion.2
  182.5 19.7 %custom-call.15 = f32[2,128,128]{1,2,0:T(8,128)S(1)} custom-call(f32[2,128,128]{2,1,0:T(8,128)S(1)} %get-tuple-element.78), custom_call_target="InvertDiagBlocksLowerTriangular" | custom-call | tf_op jit(solution)/shard_map/triangular_solve | solution.py:42
  202.9 1.0 convolution_subtract_fusion
  205.5 21.7 %all-gather.2.cloned.1.call-done = bf16[4096,256]{0,1:T(8,128)(2,1)} async-done(((bf16[1024,256]{0,1:T(8,128)(2,1)}), bf16[4096,256]{0,1:T(8,128)(2,1)}) %all-gather.2.cloned.1.call-update) | async-done | bytes 2097168 | tf_op jit(solution)/shard_map/all_gather | solution.py:46
  227.1 3.3 copy.9
  230.4 2.5 broadcast_in_dim.12
  232.9 51.8 %while.14 = (s32[]{:T(128)}, f32[8,256,512]{2,1,0:T(8,128)}, s32[]{:T(128)}, s32[40]{0:T(128)S(1)}, s32[8]{0:T(128)S(1)}, /*index=5*/s32[40]{0:T(128)S(1)}, bf16...) while((s32[]{:T(128)}, f32[8,256,512]{2,1,0:T(8,128)}, ...), condition=%wide.region_8.9_spmd, body=%wide.region_5.8_spmd.sunk | while | flops 134348832 | bytes 2884007 | solution.py:29
  238.0 5.1 conditional.2
  239.9 1.1 constant_dynamic-slice_fusion
  241.0 2.2 fusion.1
  248.2 5.1 conditional.2
  250.1 1.1 constant_dynamic-slice_fusion
  251.2 2.2 fusion.1
  258.4 5.1 conditional.2
  260.3 1.1 constant_dynamic-slice_fusion
  261.4 2.2 fusion.1
  268.7 5.2 conditional.2
  270.6 1.1 constant_dynamic-slice_fusion
  271.6 2.2 fusion.1
  278.9 5.2 conditional.2
  280.8 1.1 constant_dynamic-slice_fusion
  281.9 2.2 fusion.1
  284.7 445.8 %reduce-scatter.2.cloned.1.call-done = f32[1,256,512]{2,1,0:T(8,128)} async-done(((f32[8,256,512]{2,1,0:T(8,128)}), f32[1,256,512]{2,1,0:T(8,128)}) %reduce-scatter.2.cloned.1.call-update) | async-done | bytes 524304 | tf_op jit(solution)/shard_map/reduce_scatter | solution.py:53
  (48 shorter events, 13.6 us)
Async XLA Ops:
  6.5 195.7 %copy-start = (f32[1024,256]{1,0:T(8,128)S(1)}, f32[1024,256]{1,0:T(8,128)}, u32[]{:S(2)}) copy-start(f32[1024,256]{1,0:T(8,128)} %param.10) | copy-start | bytes 3145732
  6.5 134.0 %all-reduce.3.cloned.1.call-start = ((), (), s32[]{:S(2)}) async-start(), calls=%async_computation.1 | async-start | bytes 524288 | tf_op jit(solution)/shard_map/psum | solution.py:40
  10.7 216.4 %all-gather.2.cloned.1.call-start = ((), (), s32[]{:S(2)}) async-start(), calls=%async_computation.2 | async-start | bytes 2621440 | tf_op jit(solution)/shard_map/all_gather | solution.py:46
  205.4 525.2 %reduce-scatter.2.cloned.1.call-start = ((), (), s32[]{:S(2)}) async-start(), calls=%async_computation.3 | async-start | bytes 4718592 | tf_op jit(solution)/shard_map/reduce_scatter | solution.py:53
  205.4 27.5 %copy-start.1 = (s32[40]{0:T(128)S(1)}, s32[40]{0:T(128)}, u32[]{:S(2)}) copy-start(s32[40]{0:T(128)} %param.13) | copy-start | bytes 484
  205.4 27.5 %copy-start.2 = (s32[1,8]{1,0:T(1,128)S(1)}, s32[1,8]{1,0:T(1,128)}, u32[]{:S(2)}) copy-start(s32[1,8]{1,0:T(1,128)} %param.15) | copy-start | bytes 100
  205.5 27.4 %copy-start.3 = (s32[40]{0:T(128)S(1)}, s32[40]{0:T(128)}, u32[]{:S(2)}) copy-start(s32[40]{0:T(128)} %param.12) | copy-start | bytes 484
Sparse Core Ops, SparseCore 0:
  12.9 127.5 all-reduce.2
  205.5 21.5 all-gather.1
  284.9 445.6 reduce-scatter.1
where the time goes:
time: 744 us; the launch traced here: 737 us
  waiting for transfers between devices  597 us (80%)
  other arithmetic  55.5 us (7%)
  loops' own time  26.9 us (4%)
  local copies, waits for them, and re-layouts  25.1 us (3%)
  matrix products  17.7 us (2%)
  between operations  14.5 us (2%)
    reduce_scatter x1, waiting for transfers between devices, body(): owned = lax.psum_scatter(totals, 'rows', scatter_dimension=0, tiled=True)  446 us
    psum x1, waiting for transfers between devices, body(): total = lax.psum(gram, ('rows', 'cols'))  130 us
    another operation x6, other arithmetic, body(): lower_factor = jnp.linalg.cholesky(total)  34 us
    all_gather x1, waiting for transfers between devices, body(): slab = lax.all_gather(basis, 'cols', axis=0, tiled=True)  21.7 us
    another operation x5, other arithmetic, body(): lax.linalg.triangular_solve(lower_factor, sketch, left_side=False, lower=...  20.6 us
    another operation x1, loops' own time, accumulate(): return lax.fori_loop(0, stop, step, totals)  20.2 us
  transfers between devices with their start and end apart: 3, of which 3 were waited for; matrix products, arithmetic and copies ran while one was open for 0% of the time, Pallas kernels for 0%

commit v1 on v0

--- a/solution.py
+++ b/solution.py
@@ -37,7 +37,8 @@
         precision=lax.Precision.HIGHEST,
         preferred_element_type=jnp.float32,
     )
-    total = lax.psum(gram, ("rows", "cols"))
+    parts = lax.all_gather(gram, ("rows", "cols"), axis=0, tiled=False)
+    total = parts.sum(axis=0)
     lower_factor = jnp.linalg.cholesky(total)
     basis_full = lax.linalg.triangular_solve(
         lower_factor, sketch, left_side=False, lower=True, transpose_a=True

time: 744 us -> 696 us (0.935)
  waiting for transfers between devices: 597 us -> 547 us
    psum x1 -> x0, waiting for transfers between devices: 130 us -> none  [body(): total = lax.psum(gram, ('rows', 'cols'))]
    all_gather x0 -> x1, waiting for transfers between devices: none -> 80.2 us  [body(): parts = lax.all_gather(gram, ('rows', 'cols'), axis=0, tiled=False)]
where the time goes in v1:
time: 696 us; the launch traced here: 689 us
  waiting for transfers between devices  547 us (79%)
  other arithmetic  58.6 us (8%)
  loops' own time  26.9 us (4%)
  local copies, waits for them, and re-layouts  24.1 us (3%)
  matrix products  17.7 us (3%)
  between operations  14.5 us (2%)
    reduce_scatter x1, waiting for transfers between devices, body(): owned = lax.psum_scatter(totals, 'rows', scatter_dimension=0, tiled=True)  446 us
    all_gather x1, waiting for transfers between devices, body(): parts = lax.all_gather(gram, ('rows', 'cols'), axis=0, tiled=False)  80.2 us
    another operation x6, other arithmetic, body(): lower_factor = jnp.linalg.cholesky(total)  34 us
    all_gather x1, waiting for transfers between devices, body(): slab = lax.all_gather(basis, 'cols', axis=0, tiled=True)  21.2 us
    another operation x5, other arithmetic, body(): lax.linalg.triangular_solve(lower_factor, sketch, left_side=False, lower=...  20.6 us
    another operation x1, loops' own time, accumulate(): return lax.fori_loop(0, stop, step, totals)  20.2 us
  transfers between devices with their start and end apart: 3, of which 3 were waited for; matrix products, arithmetic and copies ran while one was open for 0% of the time, Pallas kernels for 0%

profile of v1, /device:TPU:0, one launch (start us, length us, event | category | flops | bytes accessed | tf_op | source)
XLA Modules:
  0.0 689.2 jit_solution(13729971890113179211)
XLA Ops:
  6.5 4.1 fusion.14
  10.7 80.2 %all-gather.6.cloned.1.call-done = f32[8192,256]{1,0:T(8,128)} async-done(((f32[256,256]{1,0:T(8,128)}), f32[8192,256]{1,0:T(8,128)}) %all-gather.6.cloned.1.call-update) | async-done | bytes 8388624 | tf_op jit(solution)/shard_map/all_gather | solution.py:40
  90.9 4.0 reduce_sum.9
  95.1 11.7 %cholesky.50 = f32[128,128]{1,0:T(8,128)S(1)} custom-call(f32[128,128]{1,0:T(8,128)S(1)} %cholesky.118), custom_call_target="Cholesky" | custom-call | tf_op jit(solution)/shard_map/jit(cholesky)/cholesky | solution.py:42
  106.9 9.8 %custom-call.14 = f32[1,128,128]{1,2,0:T(8,128)S(1)} custom-call(f32[1,128,128]{2,1,0:T(8,128)S(1)} %get-tuple-element.124), custom_call_target="InvertDiagBlocksLowerTriangular" | custom-call | tf_op jit(solution)/shard_map/jit(cholesky)/cholesky | solution.py:42
  117.2 11.7 %cholesky.105 = f32[128,128]{1,0:T(8,128)S(1)} custom-call(f32[128,128]{1,0:T(8,128)S(1)} %convolution_subtract_fusion.1), custom_call_target="Cholesky" | custom-call | tf_op jit(solution)/shard_map/jit(cholesky)/cholesky | solution.py:42
  131.0 4.1 while.15
  131.7 1.4 bitcast_dynamic-update-slice_fusion.2
  133.7 1.4 bitcast_dynamic-update-slice_fusion.2
  135.1 19.7 %custom-call.15 = f32[2,128,128]{1,2,0:T(8,128)S(1)} custom-call(f32[2,128,128]{2,1,0:T(8,128)S(1)} %get-tuple-element.78), custom_call_target="InvertDiagBlocksLowerTriangular" | custom-call | tf_op jit(solution)/shard_map/triangular_solve | solution.py:43
  155.4 1.0 convolution_subtract_fusion
  157.1 0.8 pad_maximum_fusion
  158.0 21.2 %all-gather.4.cloned.1.call-done = bf16[4096,256]{0,1:T(8,128)(2,1)} async-done(((bf16[1024,256]{0,1:T(8,128)(2,1)}), bf16[4096,256]{0,1:T(8,128)(2,1)}) %all-gather.4.cloned.1.call-update) | async-done | bytes 2097168 | tf_op jit(solution)/shard_map/all_gather | solution.py:47
  179.3 3.3 copy.10
  182.5 2.5 broadcast_in_dim.12
  185.0 51.8 %while.14 = (s32[]{:T(128)}, f32[8,256,512]{2,1,0:T(8,128)}, s32[]{:T(128)}, s32[40]{0:T(128)S(1)}, s32[8]{0:T(128)S(1)}, /*index=5*/s32[40]{0:T(128)S(1)}, bf16...) while((s32[]{:T(128)}, f32[8,256,512]{2,1,0:T(8,128)}, ...), condition=%wide.region_8.9_spmd, body=%wide.region_5.8_spmd.sunk | while | flops 134348832 | bytes 2884007 | solution.py:29
  190.1 5.1 conditional.2
  192.0 1.1 constant_dynamic-slice_fusion
  193.1 2.2 fusion.1
  200.3 5.1 conditional.2
  202.2 1.1 constant_dynamic-slice_fusion
  203.3 2.2 fusion.1
  210.6 5.1 conditional.2
  212.5 1.1 constant_dynamic-slice_fusion
  213.5 2.2 fusion.1
  220.8 5.2 conditional.2
  222.7 1.1 constant_dynamic-slice_fusion
  223.8 2.2 fusion.1
  231.0 5.2 conditional.2
  232.9 1.1 constant_dynamic-slice_fusion
  234.0 2.2 fusion.1
  236.9 445.8 %reduce-scatter.2.cloned.1.call-done = f32[1,256,512]{2,1,0:T(8,128)} async-done(((f32[8,256,512]{2,1,0:T(8,128)}), f32[1,256,512]{2,1,0:T(8,128)}) %reduce-scatter.2.cloned.1.call-update) | async-done | bytes 524304 | tf_op jit(solution)/shard_map/reduce_scatter | solution.py:54
  (49 shorter events, 13.0 us)
Async XLA Ops:
  6.5 84.4 %all-gather.6.cloned.1.call-start = ((), (), s32[]{:S(2)}) async-start(), calls=%async_computation.3 | async-start | bytes 8650752 | tf_op jit(solution)/shard_map/all_gather | solution.py:40
  10.6 168.6 %all-gather.4.cloned.1.call-start = ((), (), s32[]{:S(2)}) async-start(), calls=%async_computation.1 | async-start | bytes 2621440 | tf_op jit(solution)/shard_map/all_gather | solution.py:47
  90.9 63.8 %copy-start = (f32[1024,256]{1,0:T(8,128)S(1)}, f32[1024,256]{1,0:T(8,128)}, u32[]{:S(2)}) copy-start(f32[1024,256]{1,0:T(8,128)} %param.10) | copy-start | bytes 3145732
  157.9 524.8 %reduce-scatter.2.cloned.1.call-start = ((), (), s32[]{:S(2)}) async-start(), calls=%async_computation.2 | async-start | bytes 4718592 | tf_op jit(solution)/shard_map/reduce_scatter | solution.py:54
  158.0 27.0 %copy-start.1 = (s32[40]{0:T(128)S(1)}, s32[40]{0:T(128)}, u32[]{:S(2)}) copy-start(s32[40]{0:T(128)} %param.13) | copy-start | bytes 484
  158.0 27.0 %copy-start.2 = (s32[1,8]{1,0:T(1,128)S(1)}, s32[1,8]{1,0:T(1,128)}, u32[]{:S(2)}) copy-start(s32[1,8]{1,0:T(1,128)} %param.15) | copy-start | bytes 100
  158.0 27.0 %copy-start.3 = (s32[40]{0:T(128)S(1)}, s32[40]{0:T(128)}, u32[]{:S(2)}) copy-start(s32[40]{0:T(128)} %param.12) | copy-start | bytes 484
Sparse Core Ops, SparseCore 0:
  10.7 80.1 all-gather.5
  158.1 21.1 all-gather.3
  237.0 445.6 reduce-scatter.1
